TPU v7x, 32 devices: a whole 2x2x4 slice. The times are simulated.
32 devices in a mesh: dp: 2 (over x), seq: 4 (over z), tensor: 4 (over y, core).
Axes of the slice: x: 2, y: 2, z: 4, core: 2. Of those that a mesh axis runs over, the one named last changes fastest.
Arguments:
- tokens: bfloat16 [2, 4, 1024, 768], P('dp', 'seq'), may hold values from -6 to 6
- branch: int32 [2, 4], P('dp', 'seq'), may hold values from 1024 to 2048, as said below
- w_attn: bfloat16 [3, 768, 768], P(None, None, 'tensor'), may hold values from -0.3125 to 0.3125
- w_proj: bfloat16 [768, 768], P('tensor'), may hold values from -6 to 6
- w_expand: bfloat16 [768, 3072], P(None, 'tensor'), may hold values from -0.21875 to 0.21875
- w_contract: bfloat16 [3072, 768], P('tensor'), may hold values from -0.4375 to 0.4375
- attn_bias: float32 [2, 768], P(None, 'tensor'), may hold values from -3 to 3
- branch_bias: float32 [2, 768], replicated, may hold values from -4 to 4
- expand_bias: float32 [3072], P('tensor'), may hold values from -3 to 3
- norm_gains: float32 [2, 768], replicated, may hold values from 0.5 to 1.5
- norm_shifts: float32 [2, 768], replicated, may hold values from -3 to 3
- cotangent: bfloat16 [2, 4, 1024, 768], P('dp', 'seq'), may hold values from -6 to 6
Outputs:
- layer_out: bfloat16 [2, 4, 1024, 768], P('dp', 'seq', 'tensor')
- grad_tokens: bfloat16 [2, 4, 1024, 768], P('dp', 'seq', 'tensor')
- grad_attn: float32 [3, 768, 768], P(None, ('dp', 'seq'), 'tensor')
- grad_proj: float32 [768, 768], P('tensor', ('dp', 'seq'))
- grad_expand: float32 [768, 3072], P(('dp', 'seq'), 'tensor')
- grad_contract: float32 [3072, 768], P('tensor', ('dp', 'seq'))
- grad_attn_bias: float32 [2, 768], P(None, 'tensor')
- grad_branch_bias: float32 [2, 768], replicated
- grad_expand_bias: float32 [3072], P('tensor')
- grad_norm_gains: float32 [2, 768], replicated
- grad_norm_shifts: float32 [2, 768], replicated
Inputs may be any that keep to these rules, and one draw needn't show every extreme that they name: branch[g, 0] equals 2048 in every group: the first continuation sees the whole prompt.
All inputs are finite; a program needn't handle non-finite values.
Results may differ from a plain program's by a relative error of at most 0.013.
The roundings to bfloat16 on the way count: a program that leaves them out, or rounds other values in their place, can miss the bound.
Values may be sent and summed in bfloat16 or wider, within the bound.
A program may use at most 192 MiB of HBM per device.

v0:
```python
import math
import jax
import jax.numpy as jnp
from jax import lax
from jax.sharding import PartitionSpec as P

HEAD_DIM = 64
LAYERS = 12
PCH = 512
CLEN = 512
norm_eps = 1e-05
big_negative = -1000000000.0


def layer_norm(value, gain, shift):
    centre = jnp.mean(value, axis=-1, keepdims=True)
    centred = value - centre
    spread = jnp.mean(centred * centred, axis=-1, keepdims=True)
    return centred * lax.rsqrt(spread + norm_eps) * gain + shift


def scores_of(queries, all_keys, allowed, score_scale):
    raw = (
        jnp.einsum("ihd,jhd->hij", queries, all_keys, preferred_element_type=jnp.float32)
        * score_scale
    )
    return jnp.where(allowed[None], raw, big_negative)


def attend(queries, all_keys, all_values, allowed, score_scale):
    scores = scores_of(queries, all_keys, allowed, score_scale)
    highest_score = jnp.max(scores, axis=-1, keepdims=True)
    exponent = jnp.exp(scores - highest_score)
    totals = jnp.sum(exponent, axis=-1, keepdims=True)
    chances = (exponent / totals).astype(jnp.bfloat16)
    result = jnp.einsum("hij,jhd->ihd", chances, all_values, preferred_element_type=jnp.float32)
    return (result, highest_score + jnp.log(totals))


def attend_back(queries, all_keys, all_values, allowed, score_scale, logsum, grad_result):
    scores = scores_of(queries, all_keys, allowed, score_scale)
    chances = jnp.exp(scores - logsum)
    grad_chances = jnp.einsum(
        "ihd,jhd->hij", grad_result, all_values, preferred_element_type=jnp.float32
    )
    row_dot = jnp.sum(chances * grad_chances, axis=-1, keepdims=True)
    grad_scores = (chances * (grad_chances - row_dot)).astype(jnp.bfloat16)
    grad_values = jnp.einsum(
        "hij,ihd->jhd",
        chances.astype(jnp.bfloat16),
        grad_result,
        preferred_element_type=jnp.float32,
    )
    grad_queries = (
        jnp.einsum("hij,jhd->ihd", grad_scores, all_keys, preferred_element_type=jnp.float32)
        * score_scale
    )
    grad_keys = (
        jnp.einsum("hij,ihd->jhd", grad_scores, queries, preferred_element_type=jnp.float32)
        * score_scale
    )
    return (grad_queries, grad_keys, grad_values)


def gelu_tanh(inner):
    return jax.nn.gelu(inner, approximate=True)


def shards(
    tokens,
    branch,
    w_attn,
    w_proj,
    w_expand,
    w_contract,
    attn_bias,
    branch_bias,
    expand_bias,
    norm_gains,
    norm_shifts,
    cotangent,
):
    seq_count = lax.axis_size("seq")
    seq_index = lax.axis_index("seq")
    tensor_count = lax.axis_size("tensor")
    tensor_index = lax.axis_index("tensor")
    width = tokens.shape[3]
    row_count = tokens.shape[2]
    share = row_count // tensor_count
    row_start = tensor_index * share
    local_width = w_attn.shape[2]
    local_heads = local_width // HEAD_DIM
    prompt = PCH * seq_count
    score_scale = 1.0 / math.sqrt(HEAD_DIM)
    layer_scale = 1.0 / math.sqrt(LAYERS)

    def rows_of(whole):
        return lax.dynamic_slice_in_dim(whole, row_start, share, 0)

    flat_rows = tokens.reshape(row_count, width).astype(jnp.float32)
    grad_out = cotangent.reshape(row_count, width).astype(jnp.float32)
    normed_one = layer_norm(flat_rows, norm_gains[0], norm_shifts[0]).astype(jnp.bfloat16)
    projected = jnp.einsum("rd,cde->cre", normed_one, w_attn, preferred_element_type=jnp.float32)
    bias_rows = jnp.stack([attn_bias[0], jnp.zeros_like(attn_bias[0]), attn_bias[1]])
    projected = (projected + bias_rows[:, None, :]).astype(jnp.bfloat16)
    query_flat, key_flat, value_flat = (projected[0], projected[1], projected[2])
    gathered_keys, gathered_values = (
        lax.all_gather(key_flat[:PCH], "seq", axis=0, tiled=True),
        lax.all_gather(value_flat[:PCH], "seq", axis=0, tiled=True),
    )

    def heads_of(flat):
        return flat.reshape(flat.shape[0], local_heads, HEAD_DIM)

    query_prompt = heads_of(query_flat[:PCH])
    query_cont = heads_of(query_flat[PCH:])
    places = jnp.arange(prompt)
    positions = seq_index * PCH + jnp.arange(PCH)
    allowed_prompt = places[None, :] <= positions[:, None]
    cont_places = jnp.arange(CLEN)
    branch_end = branch[0, 0]
    allowed_cont = jnp.concatenate(
        [
            jnp.broadcast_to(places[None, :] < branch_end, (CLEN, prompt)),
            cont_places[None, :] <= cont_places[:, None],
        ],
        axis=1,
    )
    keys_prompt = heads_of(gathered_keys)
    values_prompt = heads_of(gathered_values)
    keys_cont = jnp.concatenate([keys_prompt, heads_of(key_flat[PCH:])], axis=0)
    values_cont = jnp.concatenate([values_prompt, heads_of(value_flat[PCH:])], axis=0)
    keys_prompt, values_prompt, keys_cont, values_cont = (
        keys_prompt,
        values_prompt,
        keys_cont,
        values_cont,
    )
    out_prompt, logsum_prompt = attend(
        query_prompt, keys_prompt, values_prompt, allowed_prompt, score_scale
    )
    out_cont, logsum_cont = attend(query_cont, keys_cont, values_cont, allowed_cont, score_scale)
    attended = (
        jnp.concatenate([out_prompt, out_cont], axis=0)
        .reshape(row_count, local_width)
        .astype(jnp.bfloat16)
    )
    attn_terms = jnp.dot(attended, w_proj, preferred_element_type=jnp.float32)
    attn_summed = lax.psum(attn_terms, "tensor")
    hidden = flat_rows + layer_scale * (attn_summed + branch_bias[0])
    normed_two = layer_norm(hidden, norm_gains[1], norm_shifts[1]).astype(jnp.bfloat16)
    preact = jnp.dot(normed_two, w_expand, preferred_element_type=jnp.float32) + expand_bias
    activated = gelu_tanh(preact).astype(jnp.bfloat16)
    contract_terms = jnp.dot(activated, w_contract, preferred_element_type=jnp.float32)
    mlp_summed = lax.psum(contract_terms.astype(jnp.bfloat16), "tensor").astype(jnp.float32)
    layer_out = rows_of((hidden + layer_scale * (mlp_summed + branch_bias[1])).astype(jnp.bfloat16))
    grad_mlp = (grad_out * layer_scale).astype(jnp.bfloat16)
    grad_contract = jnp.einsum("rf,rd->fd", activated, grad_mlp, preferred_element_type=jnp.float32)
    grad_activated = jnp.einsum(
        "rd,fd->rf", grad_mlp, w_contract, preferred_element_type=jnp.float32
    )
    gelu_value, gelu_back = jax.vjp(gelu_tanh, preact)
    grad_preact = gelu_back(grad_activated)[0].astype(jnp.bfloat16)
    grad_expand = jnp.einsum(
        "rd,rf->df", normed_two, grad_preact, preferred_element_type=jnp.float32
    )
    mixed_terms = jnp.einsum("rf,df->rd", grad_preact, w_expand, preferred_element_type=jnp.float32)
    grad_mixed = lax.psum(mixed_terms, "tensor")
    norm_value_two, norm_back_two = jax.vjp(layer_norm, hidden, norm_gains[1], norm_shifts[1])
    grad_hidden_norm, gain_two, shift_two = norm_back_two(grad_mixed)
    grad_hidden = grad_out + grad_hidden_norm
    grad_att = (grad_hidden * layer_scale).astype(jnp.bfloat16)
    grad_proj = jnp.einsum("re,rd->ed", attended, grad_att, preferred_element_type=jnp.float32)
    grad_attended = jnp.einsum(
        "rd,ed->re", grad_att, w_proj, preferred_element_type=jnp.float32
    ).astype(jnp.bfloat16)
    grad_attended = heads_of(grad_attended)
    grad_query_prompt, grad_key_pp, grad_value_pp = attend_back(
        query_prompt,
        keys_prompt,
        values_prompt,
        allowed_prompt,
        score_scale,
        logsum_prompt,
        grad_attended[:PCH],
    )
    grad_query_cont, grad_key_cont, grad_value_cont = attend_back(
        query_cont,
        keys_cont,
        values_cont,
        allowed_cont,
        score_scale,
        logsum_cont,
        grad_attended[PCH:],
    )
    prompt_key_terms = (grad_key_pp + grad_key_cont[:prompt]).reshape(prompt, local_width)
    prompt_value_terms = (grad_value_pp + grad_value_cont[:prompt]).reshape(prompt, local_width)
    own_keys, own_values = (
        lax.psum_scatter(prompt_key_terms, "seq", scatter_dimension=0, tiled=True),
        lax.psum_scatter(prompt_value_terms, "seq", scatter_dimension=0, tiled=True),
    )
    grad_keys = jnp.concatenate(
        [own_keys, grad_key_cont[prompt:].reshape(CLEN, local_width)], axis=0
    ).astype(jnp.bfloat16)
    grad_values = jnp.concatenate(
        [own_values, grad_value_cont[prompt:].reshape(CLEN, local_width)], axis=0
    ).astype(jnp.bfloat16)
    grad_queries = (
        jnp.concatenate([grad_query_prompt, grad_query_cont], axis=0)
        .reshape(row_count, local_width)
        .astype(jnp.bfloat16)
    )
    stacked = jnp.stack([grad_queries, grad_keys, grad_values])
    grad_attn = jnp.einsum("rd,cre->cde", normed_one, stacked, preferred_element_type=jnp.float32)
    normed_terms = jnp.einsum("cre,cde->rd", stacked, w_attn, preferred_element_type=jnp.float32)
    grad_normed = lax.psum(normed_terms, "tensor")
    norm_value_one, norm_back_one = jax.vjp(layer_norm, flat_rows, norm_gains[0], norm_shifts[0])
    grad_rows_norm, gain_one, shift_one = norm_back_one(grad_normed)
    grad_tokens = (grad_hidden + grad_rows_norm).astype(jnp.bfloat16)
    grad_tokens = rows_of(grad_tokens)
    bias_terms = jnp.stack(
        [
            jnp.sum(grad_queries.astype(jnp.float32), axis=0),
            jnp.sum(grad_values.astype(jnp.float32), axis=0),
        ]
    )
    branch_terms = jnp.stack(
        [
            jnp.sum(grad_att.astype(jnp.float32), axis=0),
            jnp.sum(grad_mlp.astype(jnp.float32), axis=0),
        ]
    )
    expand_terms = jnp.sum(grad_preact.astype(jnp.float32), axis=0)
    gain_terms = jnp.stack([gain_one, gain_two])
    shift_terms = jnp.stack([shift_one, shift_two])
    vectors = lax.psum(
        (bias_terms, branch_terms, expand_terms, gain_terms, shift_terms), ("dp", "seq")
    )
    reduced = (
        lax.psum_scatter(grad_attn, ("dp", "seq"), scatter_dimension=1, tiled=True),
        lax.psum_scatter(grad_proj, ("dp", "seq"), scatter_dimension=1, tiled=True),
        lax.psum_scatter(grad_expand, ("dp", "seq"), scatter_dimension=0, tiled=True),
        lax.psum_scatter(grad_contract, ("dp", "seq"), scatter_dimension=1, tiled=True),
    )
    out_shape = (1, 1, share, width)
    return (
        layer_out.reshape(out_shape),
        grad_tokens.reshape(out_shape),
        reduced[0],
        reduced[1],
        reduced[2],
        reduced[3],
        vectors[0],
        vectors[1],
        vectors[2],
        vectors[3],
        vectors[4],
    )


def solution(mesh):
    placed = (
        P("dp", "seq", None, None),
        P("dp", "seq"),
        P(None, None, "tensor"),
        P("tensor", None),
        P(None, "tensor"),
        P("tensor", None),
        P(None, "tensor"),
        P(),
        P("tensor"),
        P(),
        P(),
        P("dp", "seq", None, None),
    )
    return jax.shard_map(
        shards,
        mesh=mesh,
        in_specs=placed,
        out_specs=(
            P("dp", "seq", "tensor", None),
            P("dp", "seq", "tensor", None),
            P(None, ("dp", "seq"), "tensor"),
            P("tensor", ("dp", "seq")),
            P(("dp", "seq"), "tensor"),
            P("tensor", ("dp", "seq")),
            P(None, "tensor"),
            P(),
            P("tensor"),
            P(),
            P(),
        ),
        check_vma=False,
    )
```

profile of v0, /device:TPU:0, one launch (start us, length us, event | category | flops | bytes accessed | tf_op | source)
XLA Modules:
  0.0 758.0 jit_solution(15909318368735387643)
XLA Ops:
  11.3 2.0 fusion.27
  16.5 21.3 %all-gather.1 = bf16[1,2048,192]{1,2,0:T(8,128)(2,1)S(1)} all-gather(bf16[1,512,192]{1,2,0:T(8,128)(2,1)S(1)} %get-tuple-element.65), channel_id=3, replica_groups=mesh['dp'=2,'seq'=4,'tensor'=4] {'seq'}, dimensions={1}, use_global_device_ids=true | all-gather | bytes 983040 | tf_op jit(solution)/shard_map/all_gather | solution.py:108
  37.8 17.9 %all-gather = bf16[1,2048,192]{1,2,0:T(8,128)(2,1)S(1)} all-gather(bf16[1,512,192]{1,2,0:T(8,128)(2,1)S(1)} %get-tuple-element.66), channel_id=2, replica_groups=mesh['dp'=2,'seq'=4,'tensor'=4] {'seq'}, dimensions={1}, use_global_device_ids=true | all-gather | bytes 983040 | tf_op jit(solution)/shard_map/all_gather | solution.py:109
  57.2 2.7 fusion.87
  59.9 1.9 fusion.2
  61.8 2.7 copy-done.1
  64.5 3.1 fusion.62
  67.6 7.3 fusion.86
  74.9 7.7 %fusion = f32[3,512]{1,0:T(4,128)S(1)} fusion(f32[3,512,2560]{2,1,0:T(8,128)} %get-tuple-element.72, f32[3,512]{1,0:T(4,128)S(1)} %get-tuple-element.71), kind=kLoop, calls=%fused_computation.6 | loop fusion | flops 7862784 | bytes 15740928 | tf_op jit(solution)/shard_map/reduce_sum | solution.py:34
  82.7 7.1 fusion.61
  90.6 2.3 fusion.88
  94.7 66.6 %all-reduce.6.cloned.1.call-done = f32[1024,768]{1,0:T(8,128)} async-done(((f32[1024,768]{1,0:T(8,128)}), f32[1024,768]{1,0:T(8,128)}) %all-reduce.6.cloned.1.call-update) | async-done | bytes 3145744 | tf_op jit(solution)/shard_map/psum | solution.py:149
  161.3 2.5 fusion.81
  168.1 3.9 convert_reduce_fusion.1
  173.2 3.1 fusion.90
  178.4 66.6 %all-reduce.10.cloned.1.call-done = f32[1024,768]{1,0:T(8,128)} async-done(((f32[1024,768]{1,0:T(8,128)}), f32[1024,768]{1,0:T(8,128)}) %all-reduce.10.cloned.1.call-update) | async-done | bytes 3145744 | tf_op jit(solution)/shard_map/psum | solution.py:168
  245.0 4.4 multiply_reduce_fusion.2
  255.0 9.8 %fusion.19 = f32[2560,3,64]{0,2,1:T(8,128)} fusion(bf16[512,3,64]{0,2,1:T(8,128)(2,1)S(1)} %bitcast.166, f32[3,512,2560]{2,1,0:T(8,128)} %get-tuple-element.72, f32[3,512]{1,0:T(4,128)S(1)} %log_add_fusion), kind=kOutput, calls=%fused_computation.40 | convolution fusion | flops 511180800 | bytes 17897472 | tf_op jit(solution)/shard_map/hij,ihd->jhd/dot_general | solution.py:48
  264.8 8.0 %multiply_reduce_fusion = (f32[3,512]{1,0:T(4,128)}, f32[3,512,2560]{2,1,0:T(8,128)}) fusion(f32[3,512,2560]{2,1,0:T(8,128)S(1)} %bitcast.148, f32[3,512]{1,0:T(4,128)S(1)} %log_add_fusion, bf16[512,3,64]{0,2,1:T(8,128)(2,1)S(1)} %bitcast.167, bf16[512,3,64]{0,2,1:T(8,128)(2,1)S(1)} %bitcast.173, bf16[2048,3,64]{0,2,1:T(8,128)(2,1)S(1)} %bitcast.154), kind=kOutput, calls=%fused_computation.1 | convolution fusion | flops 517077504 | bytes 32649216 | tf_op jit(solution)/shard_map/ihd,jhd->hij/dot_general | solution.py:43
  272.9 8.2 %fusion.42 = f32[2048,3,64]{0,2,1:T(8,128)} fusion(bf16[512,3,64]{0,2,1:T(8,128)(2,1)S(1)} %bitcast.169, f32[3,512,2048]{2,1,0:T(8,128)} %copy-done.1, f32[3,512]{1,0:T(4,128)S(1)} %log_add_fusion.1, f32[2560,3,64]{0,2,1:T(8,128)} %fusion.19), kind=kOutput, calls=%fused_computation.69 | convolution fusion | flops 409337856 | bytes 15931392 | tf_op jit(solution)/shard_map/hij,ihd->jhd/dot_general | solution.py:48
  281.4 11.6 %multiply_convert_fusion = bf16[3,512,2560]{2,1,0:T(8,128)(2,1)S(1)} fusion(f32[3,512,2560]{2,1,0:T(8,128)} %get-tuple-element.76, f32[3,512,2560]{2,1,0:T(8,128)} %get-tuple-element.72, f32[3,512]{1,0:T(4,128)} %get-tuple-element.75, f32[3,512]{1,0:T(4,128)S(1)} %log_add_fusion), kind=kLoop, calls=%fused_computation | loop fusion | flops 15728640 | bytes 39333888 | tf_op jit(solution)/shard_map/convert_element_type | solution.py:47
  293.0 3.1 copy-done.4
  296.0 2.8 fusion.18
  298.8 6.5 multiply_reduce_fusion.1
  306.0 4.6 multiply_convert_fusion.1
  310.6 5.7 fusion.41
  316.4 5.2 convolution_convert_fusion
  321.6 3.7 convolution_bitcast_fusion.1
  325.3 6.5 fusion.50
  331.9 4.9 fusion.51
  340.7 12.6 %reduce-scatter.11.cloned.1.call-done = f32[512,192]{0,1:T(8,128)} async-done(((f32[2048,192]{0,1:T(8,128)}), f32[512,192]{0,1:T(8,128)}) %reduce-scatter.11.cloned.1.call-update) | async-done | bytes 393232 | tf_op jit(solution)/shard_map/reduce_scatter | solution.py:199
  355.0 4.4 convolution_bitcast_fusion
  360.1 3.6 fusion.47
  363.7 4.3 copy.25
  368.0 4.7 reshape.300
  372.8 5.8 fusion.52
  378.7 4.8 fusion.91
  383.5 13.8 %all-reduce.8.cloned.1.call-done = bf16[1024,768]{1,0:T(8,128)(2,1)} async-done(((bf16[1024,768]{1,0:T(8,128)(2,1)}), bf16[1024,768]{1,0:T(8,128)(2,1)}) %all-reduce.8.cloned.1.call-update) | async-done | bytes 1572880 | tf_op jit(solution)/shard_map/psum | solution.py:155
  397.3 2.1 fusion.66
  399.6 64.2 %reduce-scatter.21.cloned.1.call-done = f32[96,192]{1,0:T(8,128)} async-done(((f32[768,192]{1,0:T(8,128)}), f32[96,192]{1,0:T(8,128)}) %reduce-scatter.21.cloned.1.call-update) | async-done | bytes 73744
  465.6 68.1 %all-reduce.12.cloned.1.call-done = f32[1024,768]{1,0:T(8,128)} async-done(((f32[1024,768]{1,0:T(8,128)}), f32[1024,768]{1,0:T(8,128)}) %all-reduce.12.cloned.1.call-update) | async-done | bytes 3145744 | tf_op jit(solution)/shard_map/psum | solution.py:216
  533.7 3.0 fusion.26
  536.8 2.6 fusion.79
  539.5 38.3 %all-reduce = (f32[2,192]{1,0:T(2,128)}, f32[2,768]{1,0:T(2,128)}, f32[768]{0:T(1024)}, f32[2,768]{1,0:T(2,128)}, f32[2,768]{1,0:T(2,128)}) all-reduce(f32[2,192]{1,0:T(2,128)S(1)} %pad_maximum_fusion.11, f32[2,768]{1,0:T(2,128)S(1)} %pad_maximum_fusion.7, ...), channel_id=1, replica_groups=mesh['dp'=2,'seq'=4,'tensor'=4] {'dp','seq'}, use_global_device_ids=true, to_apply=%region_26.27 | all-reduce | flops 5760 | bytes 46080 | tf_op jit(solution)/shard_map/psum | solution.py:236
  577.7 2.3 fusion.67
  580.0 25.5 %reduce-scatter.19.cloned.1.call-done = f32[96,576]{1,0:T(8,128)} async-done(((f32[768,576]{1,0:T(8,128)}), f32[96,576]{1,0:T(8,128)}) %reduce-scatter.19.cloned.1.call-update) | async-done | bytes 221200
  607.4 70.9 %reduce-scatter.17.cloned.1.call-done = f32[768,96]{0,1:T(8,128)} async-done(((f32[768,768]{0,1:T(8,128)}), f32[768,96]{0,1:T(8,128)}) %reduce-scatter.17.cloned.1.call-update) | async-done | bytes 294928 | tf_op jit(solution)/shard_map/reduce_scatter | solution.py:243
  678.3 72.7 %reduce-scatter.15.cloned.1.call-done = f32[96,768]{1,0:T(8,128)} async-done(((f32[768,768]{1,0:T(8,128)}), f32[96,768]{1,0:T(8,128)}) %reduce-scatter.15.cloned.1.call-update) | async-done | bytes 294928 | tf_op jit(solution)/shard_map/reduce_scatter | solution.py:242
  (226 shorter events, 35.1 us)
Async XLA Ops:
  7.2 160.9 %copy-start = (bf16[768,768]{1,0:T(8,128)(2,1)S(1)}, bf16[768,768]{1,0:T(8,128)(2,1)}, u32[]{:S(2)}) copy-start(bf16[768,768]{1,0:T(8,128)(2,1)} %param.17) | copy-start | bytes 3538948
  7.2 7.0 copy-start.5
  7.2 6.9 copy-start.57
  7.2 6.9 copy-start.58
  7.2 154.1 %all-reduce.6.cloned.1.call-start = ((), (), s32[]{:S(2)}) async-start(), calls=%async_computation.6 | async-start | bytes 6291456 | tf_op jit(solution)/shard_map/psum | solution.py:149
  8.8 5.5 copy-start.62
  14.1 150.2 %copy-start.35 = (f32[768]{0:T(1024)}, f32[768]{0:T(1024)S(1)}, u32[]{:S(2)}) copy-start(f32[768]{0:T(1024)S(1)} %get-tuple-element.82) | copy-start | bytes 9220
  15.6 40.1 %copy-start.23 = (pred[512,512]{1,0:T(8,128)(4,1)S(1)}, pred[512,512]{1,0:T(8,128)(4,1)}, u32[]{:S(2)}) copy-start(pred[512,512]{1,0:T(8,128)(4,1)} %iota_compare_fusion.1) | copy-start | bytes 786436
  16.5 43.3 %copy-start.27 = (bf16[1,512,192]{1,2,0:T(8,128)(2,1)}, bf16[1,512,192]{1,2,0:T(8,128)(2,1)S(1)}, u32[]{:S(2)}) copy-start(bf16[1,512,192]{1,2,0:T(8,128)(2,1)S(1)} %get-tuple-element.61) | copy-start | bytes 589828
  16.5 51.1 %copy-start.12 = (bf16[1,512,192]{1,2,0:T(8,128)(2,1)}, bf16[1,512,192]{1,2,0:T(8,128)(2,1)S(1)}, u32[]{:S(2)}) copy-start(bf16[1,512,192]{1,2,0:T(8,128)(2,1)S(1)} %get-tuple-element.63) | copy-start | bytes 589828
  16.5 66.1 %copy-start.24 = (bf16[1,512,192]{1,2,0:T(8,128)(2,1)}, bf16[1,512,192]{1,2,0:T(8,128)(2,1)S(1)}, u32[]{:S(2)}) copy-start(bf16[1,512,192]{1,2,0:T(8,128)(2,1)S(1)} %get-tuple-element.64) | copy-start | bytes 589828
  37.8 29.8 %copy-start.9 = (bf16[1,2048,192]{1,2,0:T(8,128)(2,1)}, bf16[1,2048,192]{1,2,0:T(8,128)(2,1)S(1)}, u32[]{:S(2)}) copy-start(bf16[1,2048,192]{1,2,0:T(8,128)(2,1)S(1)} %all-gather.1) | copy-start | bytes 2359300
  61.8 5.8 copy-start.49
  74.9 7.7 %copy-start.50 = (f32[3,512]{1,0:T(4,128)}, f32[3,512]{1,0:T(4,128)S(1)}, u32[]{:S(2)}) copy-start(f32[3,512]{1,0:T(4,128)S(1)} %get-tuple-element.71) | copy-start | bytes 18436
  82.6 7.1 copy-start.51
  82.6 7.9 %copy-start.21 = (bf16[192,768]{1,0:T(8,128)(2,1)S(1)}, bf16[192,768]{1,0:T(8,128)(2,1)}, u32[]{:S(2)}) copy-start(bf16[192,768]{1,0:T(8,128)(2,1)} %param.15) | copy-start | bytes 884740
  92.9 152.1 %all-reduce.10.cloned.1.call-start = ((), (), s32[]{:S(2)}) async-start(), calls=%async_computation.8 | async-start | bytes 6291456 | tf_op jit(solution)/shard_map/psum | solution.py:168
  176.3 162.7 %reduce-scatter.13.cloned.1.call-start = ((), (), s32[]{:S(2)}) async-start(), calls=%async_computation.10 | async-start | bytes 1966080 | tf_op jit(solution)/shard_map/reduce_scatter | solution.py:200
  245.0 4.7 copy-start.8
  245.0 4.7 copy-start.32
  245.0 4.7 copy-start.36
  254.2 10.6 %slice-start = ((s8[15728640]{0:T(1024)(128)(4,1)}), s8[4194304]{0:T(1024)(128)(4,1)S(1)}, s32[]{:S(2)}) async-start(s8[15728640]{0:T(1024)(128)(4,1)} %bitcast.147), calls=%async_computation.16 | async-start | bytes 8388608
  254.9 18.0 %copy-start.14 = (bf16[512,192]{0,1:T(8,128)(2,1)}, bf16[512,192]{0,1:T(8,128)(2,1)S(1)}, u32[]{:S(2)}) copy-start(bf16[512,192]{0,1:T(8,128)(2,1)S(1)} %get-tuple-element.67) | copy-start | bytes 589828
  254.9 9.9 %slice-start.1 = ((s8[15728640]{0:T(1024)(128)(4,1)}), s8[4194304]{0:T(1024)(128)(4,1)S(1)}, s32[]{:S(2)}) async-start(s8[15728640]{0:T(1024)(128)(4,1)} %bitcast.147), calls=%async_computation.17 | async-start | bytes 8388608
  254.9 9.9 %slice-start.2 = ((s8[15728640]{0:T(1024)(128)(4,1)}), s8[4194304]{0:T(1024)(128)(4,1)S(1)}, s32[]{:S(2)}) async-start(s8[15728640]{0:T(1024)(128)(4,1)} %bitcast.147), calls=%async_computation.18 | async-start | bytes 8388608
  254.9 9.9 %slice-start.3 = ((s8[15728640]{0:T(1024)(128)(4,1)}), s8[3145728]{0:T(1024)(128)(4,1)S(1)}, s32[]{:S(2)}) async-start(s8[15728640]{0:T(1024)(128)(4,1)} %bitcast.147), calls=%async_computation.19 | async-start | bytes 6291456
  255.0 9.9 %copy-start.25 = (bf16[1,512,192]{1,2,0:T(8,128)(2,1)S(1)}, bf16[1,512,192]{1,2,0:T(8,128)(2,1)}, u32[]{:S(2)}) copy-start(bf16[1,512,192]{1,2,0:T(8,128)(2,1)} %copy-done.24) | copy-start | bytes 589828
  281.2 72.2 %reduce-scatter.11.cloned.1.call-start = ((), (), s32[]{:S(2)}) async-start(), calls=%async_computation.9 | async-start | bytes 1966080 | tf_op jit(solution)/shard_map/reduce_scatter | solution.py:199
  281.4 14.6 %copy-start.13 = (bf16[1,512,192]{1,2,0:T(8,128)(2,1)S(1)}, bf16[1,512,192]{1,2,0:T(8,128)(2,1)}, u32[]{:S(2)}) copy-start(bf16[1,512,192]{1,2,0:T(8,128)(2,1)} %copy-done.12) | copy-start | bytes 589828
  296.0 9.3 %slice-start.4 = ((s8[12582912]{0:T(1024)(128)(4,1)}), s8[4194304]{0:T(1024)(128)(4,1)S(1)}, s32[]{:S(2)}) async-start(s8[12582912]{0:T(1024)(128)(4,1)} %bitcast.149), calls=%async_computation.20 | async-start | bytes 8388608
  298.8 6.5 slice-start.5
  298.8 7.2 slice-start.6
  310.6 5.8 copy-start.64
  316.3 81.0 %all-reduce.8.cloned.1.call-start = ((), (), s32[]{:S(2)}) async-start(), calls=%async_computation.7 | async-start | bytes 3145728 | tf_op jit(solution)/shard_map/psum | solution.py:155
  321.6 142.2 %reduce-scatter.21.cloned.1.call-start = ((), (), s32[]{:S(2)}) async-start(), calls=%async_computation.15 | async-start | bytes 884736
  331.8 201.8 %all-reduce.12.cloned.1.call-start = ((), (), s32[]{:S(2)}) async-start(), calls=%async_computation.11 | async-start | bytes 6291456 | tf_op jit(solution)/shard_map/psum | solution.py:216
  331.9 7.0 copy-start.29
  359.5 246.0 %reduce-scatter.19.cloned.1.call-start = ((), (), s32[]{:S(2)}) async-start(), calls=%async_computation.14 | async-start | bytes 2211840
  368.0 4.8 copy-start.65
  372.7 305.6 %reduce-scatter.17.cloned.1.call-start = ((), (), s32[]{:S(2)}) async-start(), calls=%async_computation.13 | async-start | bytes 2654208 | tf_op jit(solution)/shard_map/reduce_scatter | solution.py:243
  378.6 18.7 %copy-start.52 = (f32[768]{0:T(1024)S(1)}, f32[768]{0:T(1024)}, u32[]{:S(2)}) copy-start(f32[768]{0:T(1024)} %get-tuple-element.43) | copy-start | bytes 9220
  378.6 372.3 %reduce-scatter.15.cloned.1.call-start = ((), (), s32[]{:S(2)}) async-start(), calls=%async_computation.12 | async-start | bytes 2654208 | tf_op jit(solution)/shard_map/reduce_scatter | solution.py:242
  383.5 15.9 %copy-start.54 = (f32[768]{0:T(1024)S(1)}, f32[768]{0:T(1024)}, u32[]{:S(2)}) copy-start(f32[768]{0:T(1024)} %get-tuple-element.33) | copy-start | bytes 9220
  383.5 15.9 %copy-start.53 = (f32[768]{0:T(1024)S(1)}, f32[768]{0:T(1024)}, u32[]{:S(2)}) copy-start(f32[768]{0:T(1024)} %get-tuple-element.38) | copy-start | bytes 9220
  383.5 15.9 %copy-start.56 = (f32[768]{0:T(1024)S(1)}, f32[768]{0:T(1024)}, u32[]{:S(2)}) copy-start(f32[768]{0:T(1024)} %get-tuple-element.50) | copy-start | bytes 9220
  383.5 16.0 %copy-start.55 = (f32[768]{0:T(1024)S(1)}, f32[768]{0:T(1024)}, u32[]{:S(2)}) copy-start(f32[768]{0:T(1024)} %get-tuple-element.60) | copy-start | bytes 9220
  383.5 81.9 %copy-start.16 = (f32[512,192]{0,1:T(8,128)S(1)}, f32[512,192]{0,1:T(8,128)}, u32[]{:S(2)}) copy-start(f32[512,192]{0,1:T(8,128)} %reduce-scatter.13.cloned.1.call-done) | copy-start | bytes 1179652
  399.4 137.3 %copy-start.44 = (f32[1024]{0:T(1024)S(1)}, f32[1024]{0:T(1024)}, u32[]{:S(2)}) copy-start(f32[1024]{0:T(1024)} %copy-done.43) | copy-start | bytes 12292
  (37 other events, 86.6 us)
Sparse Core Ops, SparseCore 0:
  93.0 68.2 all-reduce.5
  176.4 68.5 all-reduce.9
  281.3 35.5 reduce-scatter.12
  319.0 34.2 reduce-scatter.10
  355.5 41.6 all-reduce.7
  400.4 63.2 reduce-scatter.20
  466.1 67.4 all-reduce.11
  537.1 68.3 reduce-scatter.18
  609.6 68.6 reduce-scatter.16
  682.2 68.7 reduce-scatter.14
where the time goes:
time: 762 us; the launch traced here: 758 us
  waiting for transfers between devices  461 us (60%)
  matrix products  113 us (15%)
  blocking collectives  77.5 us (10%)
  other arithmetic  57.9 us (8%)
  local copies, waits for them, and re-layouts  31.7 us (4%)
  between operations  16 us (2%)
    unnamed x12, waiting for transfers between devices  89.8 us
    reduce_scatter x1, waiting for transfers between devices, shards(): lax.psum_scatter(grad_expand, ('dp', 'seq'), scatter_dimension=0, tiled=T...  72.7 us
    reduce_scatter x1, waiting for transfers between devices, shards(): lax.psum_scatter(grad_contract, ('dp', 'seq'), scatter_dimension=1, tiled...  70.9 us
    psum x1, waiting for transfers between devices, shards(): grad_normed = lax.psum(normed_terms, 'tensor')  68.1 us
    psum x1, waiting for transfers between devices, shards(): attn_summed = lax.psum(attn_terms, 'tensor')  66.6 us
    psum x1, waiting for transfers between devices, shards(): grad_mixed = lax.psum(mixed_terms, 'tensor')  66.6 us
    psum x1, blocking collectives, shards(): lax.psum((bias_terms, branch_terms, expand_terms, gain_terms, shift_terms...  38.3 us
    unnamed x155, local copies, waits for them, and re-layouts  26.4 us
  transfers between devices with their start and end apart: 10, of which 9 were waited for; matrix products, arithmetic and copies ran while one was open for 13% of the time, Pallas kernels for 0%

commit v1 on v0

--- a/solution.py
+++ b/solution.py
@@ -10,6 +10,22 @@
 CLEN = 512
 norm_eps = 1e-05
 big_negative = -1000000000.0
+
+
+def gather_around(x, axis, dim):
+    ways, here, turn = (lax.axis_size(axis), lax.axis_index(axis), x.shape[dim])
+    lengths = [n * ways if d == dim else n for d, n in enumerate(x.shape)]
+    full = lax.dynamic_update_slice_in_dim(jnp.zeros(lengths, x.dtype), x, here * turn, axis=dim)
+    going_up = going_down = x
+    for far in range(1, ways // 2 + 1):
+        going_up = lax.ppermute(going_up, axis, [(d, (d + 1) % ways) for d in range(ways)])
+        full = lax.dynamic_update_slice_in_dim(full, going_up, (here - far) % ways * turn, axis=dim)
+        if 2 * far < ways:
+            going_down = lax.ppermute(going_down, axis, [(d, (d - 1) % ways) for d in range(ways)])
+            full = lax.dynamic_update_slice_in_dim(
+                full, going_down, (here + far) % ways * turn, axis=dim
+            )
+    return full
 
 
 def layer_norm(value, gain, shift):
@@ -106,7 +122,7 @@
     query_flat, key_flat, value_flat = (projected[0], projected[1], projected[2])
     gathered_keys, gathered_values = (
         lax.all_gather(key_flat[:PCH], "seq", axis=0, tiled=True),
-        lax.all_gather(value_flat[:PCH], "seq", axis=0, tiled=True),
+        gather_around(value_flat[:PCH], "seq", 0),
     )
 
     def heads_of(flat):

time: 762 us -> 762 us (level)
  blocking collectives: 77.5 us -> 57.4 us
    all_gather x1 -> x0, blocking collectives: 17.9 us -> none  [shards(): lax.all_gather(value_flat[:PCH], 'seq', axis=0, tiled=True)]
    unnamed x155 -> x157, local copies, waits for them, and re-layouts: 26.4 us -> 27.6 us
  transfers between devices with their start and end apart: 10 -> 13, of which waited for: 9 -> 10; matrix products, arithmetic and copies ran while one was open for 13% -> 17% of each run, Pallas kernels for 0% -> 0%
where the time goes in v1:
time: 762 us; the launch traced here: 757 us
  waiting for transfers between devices  465 us (61%)
  matrix products  115 us (15%)
  other arithmetic  60.9 us (8%)
  blocking collectives  57.4 us (8%)
  local copies, waits for them, and re-layouts  36.3 us (5%)
  between operations  16 us (2%)
    unnamed x12, waiting for transfers between devices  89.9 us
    reduce_scatter x1, waiting for transfers between devices, shards(): lax.psum_scatter(grad_expand, ('dp', 'seq'), scatter_dimension=0, tiled=T...  72.8 us
    reduce_scatter x1, waiting for transfers between devices, shards(): lax.psum_scatter(grad_contract, ('dp', 'seq'), scatter_dimension=1, tiled...  70.7 us
    psum x1, waiting for transfers between devices, shards(): grad_normed = lax.psum(normed_terms, 'tensor')  68.1 us
    psum x1, waiting for transfers between devices, shards(): grad_mixed = lax.psum(mixed_terms, 'tensor')  66.6 us
    psum x1, waiting for transfers between devices, shards(): attn_summed = lax.psum(attn_terms, 'tensor')  65.4 us
    psum x1, blocking collectives, shards(): lax.psum((bias_terms, branch_terms, expand_terms, gain_terms, shift_terms...  38.3 us
    unnamed x157, local copies, waits for them, and re-layouts  27.6 us
  transfers between devices with their start and end apart: 13, of which 10 were waited for; matrix products, arithmetic and copies ran while one was open for 17% of the time, Pallas kernels for 0%

profile of v1, /device:TPU:0, one launch (start us, length us, event | category | flops | bytes accessed | tf_op | source)
XLA Modules:
  0.0 757.4 jit_solution(14261759236367637118)
XLA Ops:
  16.3 3.1 collective-permute-start
  19.3 2.0 collective-permute-start.1
  24.5 19.1 %all-gather = bf16[1,2048,192]{1,2,0:T(8,128)(2,1)S(1)} all-gather(bf16[1,512,192]{1,2,0:T(8,128)(2,1)} %get-tuple-element.65), channel_id=2, replica_groups=mesh['dp'=2,'seq'=4,'tensor'=4] {'seq'}, dimensions={1}, use_global_device_ids=true | all-gather | bytes 983040 | tf_op jit(solution)/shard_map/all_gather | solution.py:124
  45.2 4.0 fusion.87
  49.1 3.1 fusion.2
  53.7 8.2 %fusion.86 = (f32[3,512]{1,0:T(4,128)S(1)}, f32[3,512,2560]{2,1,0:T(8,128)}) fusion(bf16[512,3,64]{0,2,1:T(8,128)(2,1)S(1)} %bitcast.170, bf16[512,3,64]{0,2,1:T(8,128)(2,1)} %bitcast.183, bf16[2048,3,64]{0,2,1:T(8,128)(2,1)S(1)} %bitcast.163, pred[512,2560]{1,0:T(8,128)(4,1)S(1)} %pad_add_fusion), kind=kOutput, calls=%fused_computation.151 | convolution fusion | flops 517077504 | bytes 18225152 | tf_op jit(solution)/shard_map/ihd,jhd->hij/dot_general | solution.py:40
  61.9 8.3 %fusion = f32[3,512]{1,0:T(4,128)} fusion(f32[3,512,2560]{2,1,0:T(8,128)} %get-tuple-element.72, f32[3,512]{1,0:T(4,128)S(1)} %get-tuple-element.71), kind=kLoop, calls=%fused_computation.6 | loop fusion | flops 7862784 | bytes 15740928 | tf_op jit(solution)/shard_map/reduce_sum | solution.py:50
  73.6 5.6 collective-permute-done.2
  79.3 7.1 fusion.62
  87.3 3.4 fusion.61
  91.5 2.3 fusion.88
  95.3 65.4 %all-reduce.6.cloned.1.call-done = f32[1024,768]{1,0:T(8,128)} async-done(((f32[1024,768]{1,0:T(8,128)}), f32[1024,768]{1,0:T(8,128)}) %all-reduce.6.cloned.1.call-update) | async-done | bytes 3145744 | tf_op jit(solution)/shard_map/psum | solution.py:165
  160.6 2.5 fusion.81
  167.5 3.9 convert_reduce_fusion.1
  172.5 3.1 fusion.90
  177.7 66.6 %all-reduce.10.cloned.1.call-done = f32[1024,768]{1,0:T(8,128)} async-done(((f32[1024,768]{1,0:T(8,128)}), f32[1024,768]{1,0:T(8,128)}) %all-reduce.10.cloned.1.call-update) | async-done | bytes 3145744 | tf_op jit(solution)/shard_map/psum | solution.py:184
  244.4 4.4 multiply_reduce_fusion.2
  254.4 9.8 %fusion.19 = f32[2560,3,64]{0,2,1:T(8,128)} fusion(bf16[512,3,64]{0,2,1:T(8,128)(2,1)S(1)} %bitcast.172, f32[3,512,2560]{2,1,0:T(8,128)} %get-tuple-element.72, f32[3,512]{1,0:T(4,128)S(1)} %log_add_fusion), kind=kOutput, calls=%fused_computation.40 | convolution fusion | flops 511180800 | bytes 17897472 | tf_op jit(solution)/shard_map/hij,ihd->jhd/dot_general | solution.py:64
  264.3 8.1 %multiply_reduce_fusion = (f32[3,512]{1,0:T(4,128)}, f32[3,512,2560]{2,1,0:T(8,128)}) fusion(f32[3,512,2560]{2,1,0:T(8,128)S(1)} %bitcast.154, f32[3,512]{1,0:T(4,128)S(1)} %log_add_fusion, bf16[512,3,64]{0,2,1:T(8,128)(2,1)S(1)} %bitcast.173, bf16[512,3,64]{0,2,1:T(8,128)(2,1)S(1)} %bitcast.179, bf16[2048,3,64]{0,2,1:T(8,128)(2,1)S(1)} %bitcast.160), kind=kOutput, calls=%fused_computation.1 | convolution fusion | flops 517077504 | bytes 32649216 | tf_op jit(solution)/shard_map/ihd,jhd->hij/dot_general | solution.py:59
  272.3 8.3 %fusion.42 = f32[2048,3,64]{0,2,1:T(8,128)} fusion(bf16[512,3,64]{0,2,1:T(8,128)(2,1)S(1)} %bitcast.175, f32[3,512,2048]{2,1,0:T(8,128)} %copy-done.1, f32[3,512]{1,0:T(4,128)S(1)} %log_add_fusion.1, f32[2560,3,64]{0,2,1:T(8,128)} %fusion.19), kind=kOutput, calls=%fused_computation.69 | convolution fusion | flops 409337856 | bytes 15931392 | tf_op jit(solution)/shard_map/hij,ihd->jhd/dot_general | solution.py:64
  281.1 11.6 %multiply_convert_fusion = bf16[3,512,2560]{2,1,0:T(8,128)(2,1)S(1)} fusion(f32[3,512,2560]{2,1,0:T(8,128)} %get-tuple-element.76, f32[3,512,2560]{2,1,0:T(8,128)} %get-tuple-element.72, f32[3,512]{1,0:T(4,128)} %get-tuple-element.75, f32[3,512]{1,0:T(4,128)S(1)} %log_add_fusion), kind=kLoop, calls=%fused_computation | loop fusion | flops 15728640 | bytes 39333888 | tf_op jit(solution)/shard_map/convert_element_type | solution.py:63
  292.6 3.0 copy-done.4
  295.7 2.8 fusion.18
  298.5 6.5 multiply_reduce_fusion.1
  305.7 4.7 multiply_convert_fusion.1
  310.3 5.7 fusion.41
  316.1 5.2 convolution_convert_fusion
  321.4 3.8 convolution_bitcast_fusion.1
  325.1 6.5 fusion.50
  331.7 4.9 fusion.51
  340.5 12.3 %reduce-scatter.11.cloned.1.call-done = f32[512,192]{0,1:T(8,128)} async-done(((f32[2048,192]{0,1:T(8,128)}), f32[512,192]{0,1:T(8,128)}) %reduce-scatter.11.cloned.1.call-update) | async-done | bytes 393232 | tf_op jit(solution)/shard_map/reduce_scatter | solution.py:215
  354.5 4.4 convolution_bitcast_fusion
  359.6 3.6 fusion.47
  363.1 4.3 copy.25
  367.4 4.7 reshape.298
  372.2 5.8 fusion.52
  378.1 4.8 fusion.91
  383.0 13.8 %all-reduce.8.cloned.1.call-done = bf16[1024,768]{1,0:T(8,128)(2,1)} async-done(((bf16[1024,768]{1,0:T(8,128)(2,1)}), bf16[1024,768]{1,0:T(8,128)(2,1)}) %all-reduce.8.cloned.1.call-update) | async-done | bytes 1572880 | tf_op jit(solution)/shard_map/psum | solution.py:171
  396.7 2.1 fusion.66
  399.0 64.2 %reduce-scatter.21.cloned.1.call-done = f32[96,192]{1,0:T(8,128)} async-done(((f32[768,192]{1,0:T(8,128)}), f32[96,192]{1,0:T(8,128)}) %reduce-scatter.21.cloned.1.call-update) | async-done | bytes 73744
  465.1 68.1 %all-reduce.12.cloned.1.call-done = f32[1024,768]{1,0:T(8,128)} async-done(((f32[1024,768]{1,0:T(8,128)}), f32[1024,768]{1,0:T(8,128)}) %all-reduce.12.cloned.1.call-update) | async-done | bytes 3145744 | tf_op jit(solution)/shard_map/psum | solution.py:232
  533.2 3.0 fusion.26
  536.3 2.5 fusion.79
  538.9 38.3 %all-reduce = (f32[2,192]{1,0:T(2,128)}, f32[2,768]{1,0:T(2,128)}, f32[768]{0:T(1024)}, f32[2,768]{1,0:T(2,128)}, f32[2,768]{1,0:T(2,128)}) all-reduce(f32[2,192]{1,0:T(2,128)S(1)} %pad_maximum_fusion.11, f32[2,768]{1,0:T(2,128)S(1)} %pad_maximum_fusion.7, ...), channel_id=1, replica_groups=mesh['dp'=2,'seq'=4,'tensor'=4] {'dp','seq'}, use_global_device_ids=true, to_apply=%region_26.27 | all-reduce | flops 5760 | bytes 46080 | tf_op jit(solution)/shard_map/psum | solution.py:252
  577.2 2.3 fusion.67
  579.5 25.5 %reduce-scatter.19.cloned.1.call-done = f32[96,576]{1,0:T(8,128)} async-done(((f32[768,576]{1,0:T(8,128)}), f32[96,576]{1,0:T(8,128)}) %reduce-scatter.19.cloned.1.call-update) | async-done | bytes 221200
  606.9 70.7 %reduce-scatter.17.cloned.1.call-done = f32[768,96]{0,1:T(8,128)} async-done(((f32[768,768]{0,1:T(8,128)}), f32[768,96]{0,1:T(8,128)}) %reduce-scatter.17.cloned.1.call-update) | async-done | bytes 294928 | tf_op jit(solution)/shard_map/reduce_scatter | solution.py:259
  677.6 72.8 %reduce-scatter.15.cloned.1.call-done = f32[96,768]{1,0:T(8,128)} async-done(((f32[768,768]{1,0:T(8,128)}), f32[96,768]{1,0:T(8,128)}) %reduce-scatter.15.cloned.1.call-update) | async-done | bytes 294928 | tf_op jit(solution)/shard_map/reduce_scatter | solution.py:258
  (239 shorter events, 45.7 us)
Async XLA Ops:
  7.2 160.3 %copy-start = (bf16[768,768]{1,0:T(8,128)(2,1)S(1)}, bf16[768,768]{1,0:T(8,128)(2,1)}, u32[]{:S(2)}) copy-start(bf16[768,768]{1,0:T(8,128)(2,1)} %param.17) | copy-start | bytes 3538948
  7.2 5.5 copy-start.5
  7.2 5.4 copy-start.54
  7.2 5.4 copy-start.55
  7.2 153.4 %all-reduce.6.cloned.1.call-start = ((), (), s32[]{:S(2)}) async-start(), calls=%async_computation.6 | async-start | bytes 6291456 | tf_op jit(solution)/shard_map/psum | solution.py:165
  7.3 5.5 copy-start.59
  12.6 151.0 %copy-start.32 = (f32[768]{0:T(1024)}, f32[768]{0:T(1024)S(1)}, u32[]{:S(2)}) copy-start(f32[768]{0:T(1024)S(1)} %get-tuple-element.82) | copy-start | bytes 9220
  16.3 55.0 %collective-permute-start = (bf16[512,192]{0,1:T(8,128)(2,1)}, bf16[512,192]{0,1:T(8,128)(2,1)}, u32[]{:S(2)}, u32[]{:S(2)}) collective-permute-start(bf16[512,192]{0,1:T(8,128)(2,1)} %get-tuple-element.66), channel_id=1, source_target_pairs={{0,4},{4,8},{8,12},{12,0},{1,5},{5,9},{9,13},{13,1},{2,6},{6,10},{... | collective-permute-start | bytes 589832 | tf_op jit(solution)/shard_map/ppermute | solution.py:21
  19.3 53.2 %collective-permute-start.1 = (bf16[512,192]{0,1:T(8,128)(2,1)}, bf16[512,192]{0,1:T(8,128)(2,1)}, u32[]{:S(2)}, u32[]{:S(2)}) collective-permute-start(bf16[512,192]{0,1:T(8,128)(2,1)} %get-tuple-element.66), channel_id=1, source_target_pairs={{0,12},{4,0},{8,4},{12,8},{1,13},{5,1},{9,5},{13,9},{2,14},{6,2},{... | collective-permute-start | bytes 589832 | tf_op jit(solution)/shard_map/ppermute | solution.py:24
  43.6 10.2 %copy-start.9 = (bf16[1,2048,192]{1,2,0:T(8,128)(2,1)}, bf16[1,2048,192]{1,2,0:T(8,128)(2,1)S(1)}, u32[]{:S(2)}) copy-start(bf16[1,2048,192]{1,2,0:T(8,128)(2,1)S(1)} %all-gather) | copy-start | bytes 2359300
  49.1 30.1 %copy-start.44 = (f32[3,512]{1,0:T(4,128)}, f32[3,512]{1,0:T(4,128)S(1)}, u32[]{:S(2)}) copy-start(f32[3,512]{1,0:T(4,128)S(1)} %get-tuple-element.73) | copy-start | bytes 18436
  61.9 8.3 %copy-start.46 = (f32[3,512]{1,0:T(4,128)}, f32[3,512]{1,0:T(4,128)S(1)}, u32[]{:S(2)}) copy-start(f32[3,512]{1,0:T(4,128)S(1)} %get-tuple-element.71) | copy-start | bytes 18436
  71.3 7.9 %collective-permute-start.2 = (bf16[512,192]{0,1:T(8,128)(2,1)}, bf16[512,192]{0,1:T(8,128)(2,1)S(1)}, u32[]{:S(2)}, u32[]{:S(2)}) collective-permute-start(bf16[512,192]{0,1:T(8,128)(2,1)} %collective-permute-done), channel_id=1, source_target_pairs={{0,4},{4,8},{8,12},{12,0},{1,5},{5,9},{9,13},{13,1},{2,6},{6,10},{... | collective-permute-start | bytes 589832 | tf_op jit(solution)/shard_map/ppermute | solution.py:21
  72.5 13.9 %slice-start = ((s8[15728640]{0:T(1024)(128)(4,1)}), s8[4194304]{0:T(1024)(128)(4,1)S(1)}, s32[]{:S(2)}) async-start(s8[15728640]{0:T(1024)(128)(4,1)} %bitcast.151), calls=%async_computation.16 | async-start | bytes 8388608
  79.2 7.2 slice-start.1
  79.2 7.2 slice-start.2
  79.3 8.1 %slice-start.3 = ((s8[15728640]{0:T(1024)(128)(4,1)}), s8[3145728]{0:T(1024)(128)(4,1)S(1)}, s32[]{:S(2)}) async-start(s8[15728640]{0:T(1024)(128)(4,1)} %bitcast.151), calls=%async_computation.19 | async-start | bytes 6291456
  79.3 8.1 %copy-start.23 = (bf16[1,512,192]{1,2,0:T(8,128)(2,1)S(1)}, bf16[1,512,192]{1,2,0:T(8,128)(2,1)}, u32[]{:S(2)}) copy-start(bf16[1,512,192]{1,2,0:T(8,128)(2,1)} %get-tuple-element.64) | copy-start | bytes 589828
  79.3 8.1 %copy-start.47 = (f32[3,512]{1,0:T(4,128)S(1)}, f32[3,512]{1,0:T(4,128)}, u32[]{:S(2)}) copy-start(f32[3,512]{1,0:T(4,128)} %copy-done.46) | copy-start | bytes 18436
  79.3 8.0 %copy-start.48 = (f32[3,512]{1,0:T(4,128)S(1)}, f32[3,512]{1,0:T(4,128)}, u32[]{:S(2)}) copy-start(f32[3,512]{1,0:T(4,128)} %fusion) | copy-start | bytes 18436
  93.9 150.5 %all-reduce.10.cloned.1.call-start = ((), (), s32[]{:S(2)}) async-start(), calls=%async_computation.8 | async-start | bytes 6291456 | tf_op jit(solution)/shard_map/psum | solution.py:184
  175.6 163.2 %reduce-scatter.13.cloned.1.call-start = ((), (), s32[]{:S(2)}) async-start(), calls=%async_computation.10 | async-start | bytes 1966080 | tf_op jit(solution)/shard_map/reduce_scatter | solution.py:216
  253.6 10.6 %slice-start.4 = ((s8[15728640]{0:T(1024)(128)(4,1)}), s8[4194304]{0:T(1024)(128)(4,1)S(1)}, s32[]{:S(2)}) async-start(s8[15728640]{0:T(1024)(128)(4,1)} %bitcast.153), calls=%async_computation.20 | async-start | bytes 8388608
  254.3 18.0 %copy-start.15 = (bf16[512,192]{0,1:T(8,128)(2,1)}, bf16[512,192]{0,1:T(8,128)(2,1)S(1)}, u32[]{:S(2)}) copy-start(bf16[512,192]{0,1:T(8,128)(2,1)S(1)} %get-tuple-element.67) | copy-start | bytes 589828
  254.4 9.9 %slice-start.5 = ((s8[15728640]{0:T(1024)(128)(4,1)}), s8[4194304]{0:T(1024)(128)(4,1)S(1)}, s32[]{:S(2)}) async-start(s8[15728640]{0:T(1024)(128)(4,1)} %bitcast.153), calls=%async_computation.21 | async-start | bytes 8388608
  254.4 9.9 %slice-start.6 = ((s8[15728640]{0:T(1024)(128)(4,1)}), s8[4194304]{0:T(1024)(128)(4,1)S(1)}, s32[]{:S(2)}) async-start(s8[15728640]{0:T(1024)(128)(4,1)} %bitcast.153), calls=%async_computation.22 | async-start | bytes 8388608
  254.4 9.9 %slice-start.7 = ((s8[15728640]{0:T(1024)(128)(4,1)}), s8[3145728]{0:T(1024)(128)(4,1)S(1)}, s32[]{:S(2)}) async-start(s8[15728640]{0:T(1024)(128)(4,1)} %bitcast.153), calls=%async_computation.23 | async-start | bytes 6291456
  254.4 9.9 %copy-start.24 = (bf16[1,512,192]{1,2,0:T(8,128)(2,1)S(1)}, bf16[1,512,192]{1,2,0:T(8,128)(2,1)}, u32[]{:S(2)}) copy-start(bf16[1,512,192]{1,2,0:T(8,128)(2,1)} %get-tuple-element.64) | copy-start | bytes 589828
  280.6 72.2 %reduce-scatter.11.cloned.1.call-start = ((), (), s32[]{:S(2)}) async-start(), calls=%async_computation.9 | async-start | bytes 1966080 | tf_op jit(solution)/shard_map/reduce_scatter | solution.py:215
  281.1 14.6 %copy-start.14 = (bf16[1,512,192]{1,2,0:T(8,128)(2,1)S(1)}, bf16[1,512,192]{1,2,0:T(8,128)(2,1)}, u32[]{:S(2)}) copy-start(bf16[1,512,192]{1,2,0:T(8,128)(2,1)} %get-tuple-element.63) | copy-start | bytes 589828
  295.7 9.3 %slice-start.8 = ((s8[12582912]{0:T(1024)(128)(4,1)}), s8[4194304]{0:T(1024)(128)(4,1)S(1)}, s32[]{:S(2)}) async-start(s8[12582912]{0:T(1024)(128)(4,1)} %bitcast.155), calls=%async_computation.24 | async-start | bytes 8388608
  298.5 6.5 slice-start.9
  298.5 7.2 slice-start.10
  310.3 5.8 copy-start.61
  316.0 80.7 %all-reduce.8.cloned.1.call-start = ((), (), s32[]{:S(2)}) async-start(), calls=%async_computation.7 | async-start | bytes 3145728 | tf_op jit(solution)/shard_map/psum | solution.py:171
  321.3 141.9 %reduce-scatter.21.cloned.1.call-start = ((), (), s32[]{:S(2)}) async-start(), calls=%async_computation.15 | async-start | bytes 884736
  331.7 201.5 %all-reduce.12.cloned.1.call-start = ((), (), s32[]{:S(2)}) async-start(), calls=%async_computation.11 | async-start | bytes 6291456 | tf_op jit(solution)/shard_map/psum | solution.py:232
  331.7 7.0 copy-start.26
  358.9 246.1 %reduce-scatter.19.cloned.1.call-start = ((), (), s32[]{:S(2)}) async-start(), calls=%async_computation.14 | async-start | bytes 2211840
  372.2 305.4 %reduce-scatter.17.cloned.1.call-start = ((), (), s32[]{:S(2)}) async-start(), calls=%async_computation.13 | async-start | bytes 2654208 | tf_op jit(solution)/shard_map/reduce_scatter | solution.py:259
  378.1 18.7 %copy-start.49 = (f32[768]{0:T(1024)S(1)}, f32[768]{0:T(1024)}, u32[]{:S(2)}) copy-start(f32[768]{0:T(1024)} %get-tuple-element.43) | copy-start | bytes 9220
  378.1 372.3 %reduce-scatter.15.cloned.1.call-start = ((), (), s32[]{:S(2)}) async-start(), calls=%async_computation.12 | async-start | bytes 2654208 | tf_op jit(solution)/shard_map/reduce_scatter | solution.py:258
  382.9 15.9 %copy-start.51 = (f32[768]{0:T(1024)S(1)}, f32[768]{0:T(1024)}, u32[]{:S(2)}) copy-start(f32[768]{0:T(1024)} %get-tuple-element.33) | copy-start | bytes 9220
  382.9 15.9 %copy-start.50 = (f32[768]{0:T(1024)S(1)}, f32[768]{0:T(1024)}, u32[]{:S(2)}) copy-start(f32[768]{0:T(1024)} %get-tuple-element.38) | copy-start | bytes 9220
  382.9 16.0 %copy-start.53 = (f32[768]{0:T(1024)S(1)}, f32[768]{0:T(1024)}, u32[]{:S(2)}) copy-start(f32[768]{0:T(1024)} %get-tuple-element.50) | copy-start | bytes 9220
  382.9 16.0 %copy-start.52 = (f32[768]{0:T(1024)S(1)}, f32[768]{0:T(1024)}, u32[]{:S(2)}) copy-start(f32[768]{0:T(1024)} %get-tuple-element.60) | copy-start | bytes 9220
  382.9 82.0 %copy-start.17 = (f32[512,192]{0,1:T(8,128)S(1)}, f32[512,192]{0,1:T(8,128)}, u32[]{:S(2)}) copy-start(f32[512,192]{0,1:T(8,128)} %reduce-scatter.13.cloned.1.call-done) | copy-start | bytes 1179652
  398.8 137.4 %copy-start.41 = (f32[1024]{0:T(1024)S(1)}, f32[1024]{0:T(1024)}, u32[]{:S(2)}) copy-start(f32[1024]{0:T(1024)} %copy-done.40) | copy-start | bytes 12292
  (41 other events, 104.6 us)
Sparse Core Ops, SparseCore 0:
  94.0 66.6 all-reduce.5
  175.8 68.5 all-reduce.9
  280.7 35.5 reduce-scatter.12
  318.5 34.2 reduce-scatter.10
  355.0 41.6 all-reduce.7
  399.9 63.3 reduce-scatter.20
  465.6 67.4 all-reduce.11
  536.6 68.3 reduce-scatter.18
  609.1 68.4 reduce-scatter.16
  681.5 68.8 reduce-scatter.14
